TPU v7x, 32 devices: a whole 2x2x4 slice. The times are simulated.
32 devices in a mesh: dp: 8 (over z, y), mp: 4 (over x, core).
Axes of the slice: x: 2, y: 2, z: 4, core: 2. Of those that a mesh axis runs over, the one named last changes fastest.
Arguments:
- inputs: float32 [7168, 2304], P(('dp', 'mp')), may hold values from -16 to 16
- out_grad: float32 [7168, 2304], P(('dp', 'mp')), may hold values from -6 to 6
- segment_ids: int32 [8, 896], P('dp'), may hold values from 0 to 13, never falling along the last dimension, each value on 1 to 448 neighbouring positions
- pad_mask: int32 [8, 896], P('dp'), may hold values 0 or 1
- bit_sel: int32 [3], replicated, may hold values from 0 to 2
- w_qo: float32 [2, 2304, 2048], P(None, 'dp', 'mp'), may hold values from -1 to 1
- w_kv: float32 [2, 2304, 1024], P(None, 'dp', 'mp'), may hold values from -1 to 1
- w_mlp: float32 [3, 2304, 9216], P(None, 'dp', 'mp'), may hold values from -1 to 1
- norm_gains: float32 [9216], P(('dp', 'mp')), may hold values from -0.32 to 0.32
- m_qo: float32 [2, 2304, 2048], P(None, 'dp', 'mp'), may hold values from -0.3125 to 0.3125
- m_kv: float32 [2, 2304, 1024], P(None, 'dp', 'mp'), may hold values from -0.3125 to 0.3125
- m_mlp: float32 [3, 2304, 9216], P(None, 'dp', 'mp'), may hold values from -0.3125 to 0.3125
- m_gains: float32 [9216], P(('dp', 'mp')), may hold values from -0.3125 to 0.3125
- v_qo: float32 [2, 2304, 2048], P(None, 'dp', 'mp'), may hold values from 0.0066 to 0.105
- v_kv: float32 [2, 2304, 1024], P(None, 'dp', 'mp'), may hold values from 0.0066 to 0.105
- v_mlp: float32 [3, 2304, 9216], P(None, 'dp', 'mp'), may hold values from 0.0066 to 0.105
- v_gains: float32 [9216], P(('dp', 'mp')), may hold values from 0.0066 to 0.105
Outputs:
- outputs: float32 [7168, 2304], P(('dp', 'mp'))
- grad_in: float32 [7168, 2304], P(('dp', 'mp'))
- grad_norm: float32 [1], replicated
- new_w_qo: float32 [2, 2304, 2048], P(None, 'dp', 'mp')
- new_w_kv: float32 [2, 2304, 1024], P(None, 'dp', 'mp')
- new_w_mlp: float32 [3, 2304, 9216], P(None, 'dp', 'mp')
- new_gains: float32 [9216], P(('dp', 'mp'))
- new_m_qo: float32 [2, 2304, 2048], P(None, 'dp', 'mp')
- new_m_kv: float32 [2, 2304, 1024], P(None, 'dp', 'mp')
- new_m_mlp: float32 [3, 2304, 9216], P(None, 'dp', 'mp')
- new_m_gains: float32 [9216], P(('dp', 'mp'))
- new_v_qo: float32 [2, 2304, 2048], P(None, 'dp', 'mp')
- new_v_kv: float32 [2, 2304, 1024], P(None, 'dp', 'mp')
- new_v_mlp: float32 [3, 2304, 9216], P(None, 'dp', 'mp')
- new_v_gains: float32 [9216], P(('dp', 'mp'))
Inputs may be any that keep to these rules, and one draw needn't show every extreme that they name: `segment_ids`: ids never fall along a sequence; a document holds 1 to 448 slots, one exactly that many in each sequence.
All inputs are finite; a program needn't handle non-finite values. No bound on the sum of `pad_mask` on one device may be relied on, other than what follows from the above.
Results may differ from a plain program's by a relative error of at most 0.02.
Values may be sent and summed in bfloat16 or wider, within the bound.
A program may use at most 320 MiB of HBM per device.

v0:
```python
import math
import jax
import jax.numpy as jnp
from jax import lax
from jax.sharding import PartitionSpec as P

D = 2304
HEAD_WIDTH = 256
FF = 9216
NORMS = 4
QW = 2048
PARAMS = 77865984
EPSILON = 1e-06
SOFT_CAP = 50.0
ROPE_BASE = 10000.0
MASKED_SCORE = -1e30
FIRST_DECAY = 0.9
SECOND_DECAY = 0.95
LEARN_RATE = 0.04
WEIGHT_DECAY = 0.1
ADAM_EPSILON = 1e-08
CLIP_SCALE = 0.5


def quantize(master, fan_list, selector):
    shifts = jnp.where(selector == 0, 0, jnp.where(selector == 1, 4, 6)).astype(jnp.int32)
    spacing = jnp.left_shift(jnp.int32(1), shifts)
    step_sizes = jnp.array(
        [1.0 / (32.0 * math.sqrt(fan_in)) for fan_in in fan_list], jnp.float32
    ).reshape(-1, 1, 1)
    codes = jnp.clip(jnp.floor(master / step_sizes + 0.5), -128.0, 127.0).astype(jnp.int32)
    sliced = jnp.floor_divide(codes + spacing // 2, spacing)
    sliced = jnp.clip(sliced, -(128 // spacing), 128 // spacing - 1)
    return ((sliced * spacing).astype(jnp.float32) * step_sizes).astype(jnp.bfloat16)


def rms_norm(values, norm_gain):
    return (
        values
        * lax.rsqrt(jnp.mean(values * values, axis=-1, keepdims=True) + EPSILON)
        * (1.0 + norm_gain)
    )


def doc_positions(segments):
    slot_index = jnp.arange(segments.shape[0], dtype=jnp.int32)
    previous = jnp.concatenate([segments[:1] - 1, segments[:-1]])
    starts = segments != previous
    doc_begin = lax.cummax(jnp.where(starts, slot_index, 0), axis=0)
    return slot_index - doc_begin


def allowed_pairs(segments, padding):
    slot_index = jnp.arange(segments.shape[0], dtype=jnp.int32)
    same_doc = segments[:, None] == segments[None, :]
    causal = slot_index[None, :] <= slot_index[:, None]
    live_key = (padding[None, :] == 1) | (slot_index[None, :] == slot_index[:, None])
    return same_doc & causal & live_key


def apply_rotation(values, token_positions):
    half_dim = HEAD_WIDTH // 2
    frequency = ROPE_BASE ** (-jnp.arange(half_dim, dtype=jnp.float32) * 2.0 / HEAD_WIDTH)
    angles = token_positions.astype(jnp.float32)[:, None] * frequency[None, :]
    angles = jnp.concatenate([angles, angles], -1)
    cosine = jnp.cos(angles)[:, None, :]
    sine = jnp.sin(angles)[:, None, :]
    first_half = values[..., :half_dim]
    second = values[..., half_dim:]
    turned = jnp.concatenate([-second, first_half], -1)
    return values * cosine + turned * sine


def contract_rows(left, right):
    return lax.dot_general(
        left, right, (((0,), (0,)), ((), ())), preferred_element_type=jnp.float32
    )


def contract_cols(left, right):
    return lax.dot_general(
        left, right, (((1,), (1,)), ((), ())), preferred_element_type=jnp.float32
    )


def adam_update(master, first_moment, second_moment, gradient, factor):
    clipped = gradient * factor
    new_first = FIRST_DECAY * first_moment + (1.0 - FIRST_DECAY) * clipped
    new_second = SECOND_DECAY * second_moment + (1.0 - SECOND_DECAY) * clipped * clipped
    new_master = master - LEARN_RATE * (
        new_first / (jnp.sqrt(new_second) + ADAM_EPSILON) + WEIGHT_DECAY * master
    )
    return (new_master, new_first, new_second)


def local(
    inputs,
    out_grad,
    segment_ids,
    pad_mask,
    bit_sel,
    w_qo,
    w_kv,
    w_mlp,
    norm_gains,
    m_qo,
    m_kv,
    m_mlp,
    m_gains,
    v_qo,
    v_kv,
    v_mlp,
    v_gains,
):
    row_count = inputs.shape[0]
    seq_len = segment_ids.shape[1]
    low_qo = quantize(w_qo, (D, QW), bit_sel[0])
    low_kv = quantize(w_kv, (D, D), bit_sel[1])
    low_mlp = quantize(w_mlp, (D, D, FF), bit_sel[2])
    full_qo, full_kv, full_mlp = (
        lax.all_gather(low_qo, "dp", axis=1, tiled=True),
        lax.all_gather(low_kv, "dp", axis=1, tiled=True),
        lax.all_gather(low_mlp, "dp", axis=1, tiled=True),
    )
    gain_rows = lax.all_gather(norm_gains, ("dp", "mp"), axis=0, tiled=True).reshape(NORMS, D)
    segments = segment_ids[0]
    padding = pad_mask[0]
    token_positions = doc_positions(segments)
    allowed = allowed_pairs(segments, padding)
    local_heads = full_qo.shape[2] // HEAD_WIDTH
    kv_heads = full_kv.shape[2] // HEAD_WIDTH
    group_size = local_heads // kv_heads
    scale = HEAD_WIDTH ** (-0.5)
    normalized_rows = rms_norm(inputs, gain_rows[0]).astype(jnp.bfloat16)
    seq_normed = lax.all_gather(normalized_rows, "mp", axis=0, tiled=True)
    query_linear = jnp.dot(seq_normed, full_qo[0], preferred_element_type=jnp.float32)
    key_linear = jnp.dot(seq_normed, full_kv[0], preferred_element_type=jnp.float32)
    value_lin = jnp.dot(seq_normed, full_kv[1], preferred_element_type=jnp.float32)

    def rope_query(values):
        turned = apply_rotation(values.reshape(seq_len, local_heads, HEAD_WIDTH), token_positions)
        return turned.reshape(seq_len, kv_heads, group_size, HEAD_WIDTH)

    def rope_key(values):
        return apply_rotation(values.reshape(seq_len, kv_heads, HEAD_WIDTH), token_positions)

    query_bf = rope_query(query_linear).astype(jnp.bfloat16)
    key_bf = rope_key(key_linear).astype(jnp.bfloat16)
    value_bf = value_lin.astype(jnp.bfloat16).reshape(seq_len, kv_heads, HEAD_WIDTH)

    def masked_scores():
        raw_scores = (
            jnp.einsum("qkgd,pkd->kgqp", query_bf, key_bf, preferred_element_type=jnp.float32)
            * scale
        )
        capped = jnp.where(
            allowed[None, None], SOFT_CAP * jnp.tanh(raw_scores / SOFT_CAP), MASKED_SCORE
        )
        return (raw_scores, capped)

    raw_scores, capped = masked_scores()
    row_top = jnp.max(capped, axis=-1, keepdims=True)
    log_total = row_top + jnp.log(jnp.sum(jnp.exp(capped - row_top), axis=-1, keepdims=True))
    probs_bf = jnp.exp(capped - log_total).astype(jnp.bfloat16)
    mixed_bf = (
        jnp.einsum("kgqp,pkd->qkgd", probs_bf, value_bf, preferred_element_type=jnp.float32)
        .reshape(seq_len, -1)
        .astype(jnp.bfloat16)
    )
    row_block = mixed_bf
    attended = lax.psum_scatter(
        contract_cols(row_block, full_qo[1]), "mp", scatter_dimension=0, tiled=True
    )
    hidden_in = inputs + rms_norm(attended, gain_rows[1])
    ffn_normed = rms_norm(hidden_in, gain_rows[2]).astype(jnp.bfloat16)
    seq_ffn = lax.all_gather(ffn_normed, "mp", axis=0, tiled=True)
    gate_up = jnp.einsum("td,kdf->ktf", seq_ffn, full_mlp[:2], preferred_element_type=jnp.float32)
    activated_bf = (jax.nn.gelu(gate_up[0], approximate=True) * gate_up[1]).astype(jnp.bfloat16)
    row_block = activated_bf
    branch = lax.psum_scatter(
        contract_cols(row_block, full_mlp[2]), "mp", scatter_dimension=0, tiled=True
    )
    outputs = hidden_in + rms_norm(branch, gain_rows[3])
    row_live = lax.dynamic_slice_in_dim(
        padding, lax.axis_index("mp") * row_count, row_count
    ).astype(jnp.float32)
    cotangent = out_grad * row_live[:, None]
    _, branch_pull = jax.vjp(rms_norm, branch, gain_rows[3])
    grad_branch, grad_gain_three = branch_pull(cotangent)
    seq_grad_branch = lax.all_gather(grad_branch.astype(jnp.bfloat16), "mp", axis=0, tiled=True)
    back_qo, back_kv, back_mlp = (
        lax.all_gather(low_qo, "dp", axis=1, tiled=True),
        lax.all_gather(low_kv, "dp", axis=1, tiled=True),
        lax.all_gather(low_mlp, "dp", axis=1, tiled=True),
    )
    grad_act = jnp.dot(seq_grad_branch, back_mlp[2], preferred_element_type=jnp.float32)
    grad_down = contract_rows(seq_grad_branch, activated_bf)
    _, act_pull = jax.vjp(
        lambda gate_in, up_in: jax.nn.gelu(gate_in, approximate=True) * up_in,
        gate_up[0],
        gate_up[1],
    )
    grad_gate, grad_up = act_pull(grad_act)
    grad_gate_up = jnp.stack([grad_gate, grad_up]).astype(jnp.bfloat16)
    grad_gate_up_w = jnp.einsum(
        "ktf,td->kdf", grad_gate_up, seq_ffn, preferred_element_type=jnp.float32
    )
    row_block = grad_gate_up
    grad_ffn_normed = lax.psum_scatter(
        jnp.einsum("ktf,kdf->td", row_block, back_mlp[:2], preferred_element_type=jnp.float32),
        "mp",
        scatter_dimension=0,
        tiled=True,
    )
    _, ffn_pull = jax.vjp(rms_norm, hidden_in, gain_rows[2])
    grad_hidden_part, grad_gain_two = ffn_pull(grad_ffn_normed)
    grad_hidden = cotangent + grad_hidden_part
    _, attn_pull = jax.vjp(rms_norm, attended, gain_rows[1])
    grad_attended, grad_gain_one = attn_pull(grad_hidden)
    seq_grad_attended = lax.all_gather(grad_attended.astype(jnp.bfloat16), "mp", axis=0, tiled=True)
    grad_mixed = jnp.dot(seq_grad_attended, back_qo[1], preferred_element_type=jnp.float32)
    grad_mixed = grad_mixed.astype(jnp.bfloat16).reshape(seq_len, kv_heads, group_size, HEAD_WIDTH)
    grad_out_w = contract_rows(seq_grad_attended, mixed_bf)
    raw_scores, capped = masked_scores()
    probs = jnp.exp(capped - log_total)
    probs_bf = probs.astype(jnp.bfloat16)
    grad_value = jnp.einsum(
        "kgqp,qkgd->pkd", probs_bf, grad_mixed, preferred_element_type=jnp.float32
    )
    grad_probs = jnp.einsum(
        "qkgd,pkd->kgqp", grad_mixed, value_bf, preferred_element_type=jnp.float32
    )
    inner_sum = jnp.sum(probs * grad_probs, axis=-1, keepdims=True)
    grad_capped = probs * (grad_probs - inner_sum)
    grad_raw = (grad_capped * (1.0 - jnp.square(jnp.tanh(raw_scores / SOFT_CAP)))).astype(
        jnp.bfloat16
    )
    grad_query = (
        jnp.einsum("kgqp,pkd->qkgd", grad_raw, key_bf, preferred_element_type=jnp.float32) * scale
    )
    grad_key = (
        jnp.einsum("kgqp,qkgd->pkd", grad_raw, query_bf, preferred_element_type=jnp.float32) * scale
    )
    _, query_pull = jax.vjp(rope_query, query_linear)
    grad_query_lin = query_pull(grad_query)[0].astype(jnp.bfloat16)
    _, key_pull = jax.vjp(rope_key, key_linear)
    grad_key_lin = key_pull(grad_key)[0].astype(jnp.bfloat16)
    grad_value_lin = grad_value.reshape(seq_len, -1).astype(jnp.bfloat16)
    grad_query_w = contract_rows(seq_normed, grad_query_lin)
    grad_key_w = contract_rows(seq_normed, grad_key_lin)
    grad_value_w = contract_rows(seq_normed, grad_value_lin)
    grad_normed = lax.psum_scatter(
        contract_cols(grad_query_lin, back_qo[0])
        + contract_cols(grad_key_lin, back_kv[0])
        + contract_cols(grad_value_lin, back_kv[1]),
        "mp",
        scatter_dimension=0,
        tiled=True,
    )
    _, input_pull = jax.vjp(rms_norm, inputs, gain_rows[0])
    grad_input_part, grad_gain_zero = input_pull(grad_normed)
    grad_in = grad_hidden + grad_input_part
    sum_qo, sum_kv, sum_mlp = (
        lax.psum_scatter(
            jnp.stack([grad_query_w, grad_out_w]).astype(jnp.bfloat16),
            "dp",
            scatter_dimension=1,
            tiled=True,
        ).astype(jnp.float32),
        lax.psum_scatter(
            jnp.stack([grad_key_w, grad_value_w]).astype(jnp.bfloat16),
            "dp",
            scatter_dimension=1,
            tiled=True,
        ).astype(jnp.float32),
        lax.psum_scatter(
            jnp.concatenate([grad_gate_up_w, grad_down[None]], 0).astype(jnp.bfloat16),
            "dp",
            scatter_dimension=1,
            tiled=True,
        ).astype(jnp.float32),
    )
    gain_terms = jnp.stack([grad_gain_zero, grad_gain_one, grad_gain_two, grad_gain_three]).reshape(
        -1
    )
    sum_gains = lax.psum_scatter(gain_terms, ("dp", "mp"), scatter_dimension=0, tiled=True)
    local_squares = (
        jnp.sum(sum_qo * sum_qo)
        + jnp.sum(sum_kv * sum_kv)
        + jnp.sum(sum_mlp * sum_mlp)
        + jnp.sum(sum_gains * sum_gains)
    )
    grad_norm = jnp.sqrt(lax.psum(local_squares, ("dp", "mp")))
    factor = jnp.minimum(1.0, CLIP_SCALE * math.sqrt(PARAMS) / grad_norm)
    new_w_qo, new_m_qo, new_v_qo = adam_update(w_qo, m_qo, v_qo, sum_qo, factor)
    new_w_kv, new_m_kv, new_v_kv = adam_update(w_kv, m_kv, v_kv, sum_kv, factor)
    new_w_mlp, new_m_mlp, new_v_mlp = adam_update(w_mlp, m_mlp, v_mlp, sum_mlp, factor)
    new_gains, new_m_gains, new_v_gains = adam_update(
        norm_gains, m_gains, v_gains, sum_gains, factor
    )
    return (
        outputs,
        grad_in,
        grad_norm.reshape(1),
        new_w_qo,
        new_w_kv,
        new_w_mlp,
        new_gains,
        new_m_qo,
        new_m_kv,
        new_m_mlp,
        new_m_gains,
        new_v_qo,
        new_v_kv,
        new_v_mlp,
        new_v_gains,
    )


def solution(mesh):
    placed = (
        P(("dp", "mp"), None),
        P(("dp", "mp"), None),
        P("dp", None),
        P("dp", None),
        P(),
        P(None, "dp", "mp"),
        P(None, "dp", "mp"),
        P(None, "dp", "mp"),
        P(("dp", "mp")),
        P(None, "dp", "mp"),
        P(None, "dp", "mp"),
        P(None, "dp", "mp"),
        P(("dp", "mp")),
        P(None, "dp", "mp"),
        P(None, "dp", "mp"),
        P(None, "dp", "mp"),
        P(("dp", "mp")),
    )
    return jax.shard_map(
        local,
        mesh=mesh,
        in_specs=placed,
        out_specs=(
            P(("dp", "mp"), None),
            P(("dp", "mp"), None),
            P(),
            P(None, "dp", "mp"),
            P(None, "dp", "mp"),
            P(None, "dp", "mp"),
            P(("dp", "mp")),
            P(None, "dp", "mp"),
            P(None, "dp", "mp"),
            P(None, "dp", "mp"),
            P(("dp", "mp")),
            P(None, "dp", "mp"),
            P(None, "dp", "mp"),
            P(None, "dp", "mp"),
            P(("dp", "mp")),
        ),
        check_vma=False,
    )
```

profile of v0, /device:TPU:0, one launch (start us, length us, event | category | flops | bytes accessed | tf_op | source)
XLA Modules:
  0.0 2190.6 jit_solution(6801145849870063751)
XLA Ops:
  10.1 7.8 fusion.135
  18.9 43.8 %all-reduce.4 = f32[9216]{0:T(1024)S(1)} all-reduce(f32[9216]{0:T(1024)S(1)} %dynamic-update-slice), channel_id=1, replica_groups=mesh['dp'=8,'mp'=4] {'dp','mp'}, use_global_device_ids=true, to_apply=%add.4 | all-reduce | flops 9216 | bytes 73728
  68.5 13.4 fusion.107
  87.0 21.4 all-gather.8.cloned.1.call-done
  108.4 4.1 fusion.115
  112.6 4.6 fusion.117
  119.3 71.8 %all-gather.12.cloned.1.call-done = bf16[2,2304,512]{2,1,0:T(8,128)(2,1)} async-done(((bf16[2,288,512]{2,1,0:T(8,128)(2,1)}), bf16[2,2304,512]{2,1,0:T(8,128)(2,1)}) %all-gather.12.cloned.1.call-update) | async-done | bytes 4718608 | tf_op jit(solution)/shard_map/all_gather | solution.py:121
  191.1 3.2 slice_bitcast_fusion.6
  194.3 4.3 copy.65
  198.6 5.5 fusion.52
  212.4 5.6 fusion.75
  218.1 69.1 %reduce-scatter.8.cloned.1.call-done = f32[224,2304]{1,0:T(8,128)} async-done(((f32[896,2304]{1,0:T(8,128)}), f32[224,2304]{1,0:T(8,128)}) %reduce-scatter.8.cloned.1.call-update) | async-done | bytes 2064400 | tf_op jit(solution)/shard_map/reduce_scatter | solution.py:171
  295.2 84.8 %fusion.33 = bf16[3,288,2304]{2,1,0:T(8,128)(2,1)} fusion(f32[3,288,2304]{2,1,0:T(8,128)} %param.27, f32[3]{0:T(128)S(1)} %copy-done.54, s32[]{:T(128)} %bitcast.23, s32[]{:T(128)S(6)} %sign.50, s32[]{:T(128)S(6)} %select_n.93, f32[3]{0:T(128)S(1)} %copy-done.55, s32[]{:T(128)S(6)} %neg.36, s32[]{:T(128)S(6)} %sub.130), kind=kLoop, calls=%fused_computation.52 | loop fusion | flops 39813120 | bytes 11943980 | tf_op jit(solution)/shard_map/convert_element_type | solution.py:34
  380.1 605.9 %all-gather.14.cloned.1.call-done = bf16[3,2304,2304]{2,1,0:T(8,128)(2,1)} async-done(((bf16[3,288,2304]{2,1,0:T(8,128)(2,1)}), bf16[3,2304,2304]{2,1,0:T(8,128)(2,1)}) %all-gather.14.cloned.1.call-update) | async-done | bytes 31850512 | tf_op jit(solution)/shard_map/all_gather | solution.py:123
  985.9 28.7 %convolution_bitcast_fusion = f32[2,896,2304]{1,2,0:T(8,128)} fusion(bf16[3,2304,2304]{2,1,0:T(8,128)(2,1)} %all-gather.14.cloned.1.call-done, bf16[896,2304]{1,0:T(8,128)(2,1)} %all-gather.16.cloned.1.call-done), kind=kOutput, calls=%fused_computation.18 | convolution fusion | flops 19025362944 | bytes 52494336 | tf_op jit(solution)/shard_map/td,kdf->ktf/dot_general | solution.py:177
  1014.7 22.6 %fusion.6 = f32[896,2304]{1,0:T(8,128)} fusion(bf16[3,2304,2304]{2,1,0:T(8,128)(2,1)} %all-gather.14.cloned.1.call-done, f32[2,896,2304]{1,2,0:T(8,128)} %convolution_bitcast_fusion), kind=kOutput, calls=%fused_computation.17 | convolution fusion | flops 9533325312 | bytes 35389440 | tf_op jit(solution)/shard_map/dot_general | solution.py:81
  1037.4 70.9 %reduce-scatter.10.cloned.1.call-done = f32[224,2304]{1,0:T(8,128)} async-done(((f32[896,2304]{1,0:T(8,128)}), f32[224,2304]{1,0:T(8,128)}) %reduce-scatter.10.cloned.1.call-update) | async-done | bytes 2064400 | tf_op jit(solution)/shard_map/reduce_scatter | solution.py:180
  1110.3 3.5 multiply_reduce_fusion
  1116.5 34.2 %all-gather.18.cloned.1.call-done = bf16[896,2304]{1,0:T(8,128)(2,1)} async-done(((bf16[224,2304]{1,0:T(8,128)(2,1)}), bf16[896,2304]{1,0:T(8,128)(2,1)}) %all-gather.18.cloned.1.call-update) | async-done | bytes 4128784 | tf_op jit(solution)/shard_map/all_gather | solution.py:190
  1150.7 26.8 %fusion.58 = (bf16[1,896,2304]{1,2,0:T(8,128)(2,1)}, bf16[1,896,2304]{1,2,0:T(8,128)(2,1)}) fusion(f32[2,896,2304]{1,2,0:T(8,128)} %convolution_bitcast_fusion, bf16[896,2304]{1,0:T(8,128)(2,1)} %all-gather.18.cloned.1.call-done, bf16[3,2304,2304]{2,1,0:T(8,128)(2,1)} %all-gather.14.cloned.1.call-done), kind=kOutput, calls=%fused_computation.87 | convolution fusion | flops 9562226688 | bytes 39518208 | tf_op jit(solution)/shard_map/dot_general | solution.py:196
  1177.5 27.1 %fusion.43 = f32[896,2304]{1,0:T(8,128)} fusion(bf16[3,2304,2304]{2,1,0:T(8,128)(2,1)} %all-gather.14.cloned.1.call-done, bf16[1,896,2304]{1,2,0:T(8,128)(2,1)} %get-tuple-element.39, bf16[1,896,2304]{1,2,0:T(8,128)(2,1)} %get-tuple-element.38), kind=kOutput, calls=%fused_computation.73 | convolution fusion | flops 19029491712 | bytes 37748736 | tf_op jit(solution)/shard_map/ktf,kdf->td/dot_general | solution.py:210
  1204.7 71.0 %reduce-scatter.12.cloned.1.call-done = f32[224,2304]{1,0:T(8,128)} async-done(((f32[896,2304]{1,0:T(8,128)}), f32[224,2304]{1,0:T(8,128)}) %reduce-scatter.12.cloned.1.call-update) | async-done | bytes 2064400 | tf_op jit(solution)/shard_map/reduce_scatter | solution.py:209
  1278.5 2.9 multiply_reduce_fusion.2
  1284.2 34.2 %all-gather.20.cloned.1.call-done = bf16[896,2304]{1,0:T(8,128)(2,1)} async-done(((bf16[224,2304]{1,0:T(8,128)(2,1)}), bf16[896,2304]{1,0:T(8,128)(2,1)}) %all-gather.20.cloned.1.call-update) | async-done | bytes 4128784 | tf_op jit(solution)/shard_map/all_gather | solution.py:220
  1318.4 5.6 fusion.86
  1324.0 5.5 fusion.41
  1329.6 5.5 fusion.99
  1335.1 2.9 fusion.40
  1338.0 3.8 fusion.126
  1341.9 3.6 fusion.125
  1355.3 2.9 fusion.60
  1358.2 2.9 fusion.59
  1361.2 2.6 pad_maximum_fusion.4
  1366.9 4.1 fusion.72
  1371.0 4.5 add_add_fusion
  1375.6 20.8 fusion.3
  1396.3 29.3 %fusion.2 = bf16[2,2304,2304]{2,1,0:T(8,128)(2,1)} fusion(bf16[1,896,2304]{1,2,0:T(8,128)(2,1)} %get-tuple-element.39, bf16[1,896,2304]{1,2,0:T(8,128)(2,1)} %get-tuple-element.38, bf16[896,2304]{1,0:T(8,128)(2,1)S(1)} %copy-done.61), kind=kOutput, calls=%fused_computation.4 | convolution fusion | flops 19052494848 | bytes 33619968 | tf_op jit(solution)/shard_map/ktf,td->kdf/dot_general | solution.py:205
  1425.6 22.0 %pad_maximum_fusion = bf16[3,2304,2304]{2,1,0:T(8,128)(2,1)} fusion(bf16[1,2304,2304]{2,1,0:T(8,128)(2,1)} %fusion.3, bf16[2,2304,2304]{2,1,0:T(8,128)(2,1)} %fusion.2), kind=kLoop, calls=%fused_computation | loop fusion | flops 15925248 | bytes 63700992 | tf_op jit(solution)/shard_map/concatenate | solution.py:277
  1450.2 67.4 %reduce-scatter.16.cloned.1.call-done = bf16[2,288,512]{2,1,0:T(8,128)(2,1)} async-done(((bf16[2,2304,512]{2,1,0:T(8,128)(2,1)}), bf16[2,288,512]{2,1,0:T(8,128)(2,1)}) %reduce-scatter.16.cloned.1.call-update) | async-done | bytes 589840 | tf_op jit(solution)/shard_map/reduce_scatter | solution.py:264
  1520.9 70.1 %reduce-scatter.14.cloned.1.call-done = f32[224,2304]{1,0:T(8,128)} async-done(((f32[896,2304]{1,0:T(8,128)}), f32[224,2304]{1,0:T(8,128)}) %reduce-scatter.14.cloned.1.call-update) | async-done | bytes 2064400 | tf_op jit(solution)/shard_map/reduce_scatter | solution.py:252
  1593.1 44.4 %all-reduce.5 = f32[9216]{0:T(1024)S(1)} all-reduce(f32[9216]{0:T(1024)S(1)} %reshape.540), channel_id=9, replica_groups=mesh['dp'=8,'mp'=4] {'dp','mp'}, use_global_device_ids=true, to_apply=%region_27.28.clone | all-reduce | flops 9216 | bytes 73728
  1638.3 470.0 %reduce-scatter.20.cloned.1.call-done = bf16[3,288,2304]{2,1,0:T(8,128)(2,1)} async-done(((bf16[3,2304,2304]{2,1,0:T(8,128)(2,1)}), bf16[3,288,2304]{2,1,0:T(8,128)(2,1)}) %reduce-scatter.20.cloned.1.call-update) | async-done | bytes 3981328 | tf_op jit(solution)/shard_map/reduce_scatter | solution.py:276
  2108.3 4.8 fusion.27
  2114.4 4.0 fusion.80
  2118.4 39.6 %psum.7 = f32[]{:T(128)} all-reduce(f32[]{:T(128)S(6)} %add.301), channel_id=1, replica_groups=mesh['dp'=8,'mp'=4] {'dp','mp'}, use_global_device_ids=true, to_apply=%region_29.30 | all-reduce | flops 1 | bytes 8 | tf_op jit(solution)/shard_map/psum | solution.py:293
  2159.5 4.6 multiply_subtract_fusion.1
  2164.1 2.7 multiply_subtract_fusion.2
  2166.8 15.6 multiply_subtract_fusion
  (237 shorter events, 59.3 us)
Async XLA Ops:
  7.2 61.3 %copy-start.56 = (f32[2]{0:T(128)S(1)}, f32[2]{0:T(128)}, u32[]{:S(2)}) copy-start(f32[2]{0:T(128)} %constant.220) | copy-start | bytes 28
  7.2 61.3 %copy-start.57 = (f32[2]{0:T(128)S(1)}, f32[2]{0:T(128)}, u32[]{:S(2)}) copy-start(f32[2]{0:T(128)} %constant.206.clone) | copy-start | bytes 28
  7.2 58.4 %copy-start = (f32[224,2304]{1,0:T(8,128)S(1)}, f32[224,2304]{1,0:T(8,128)}, u32[]{:S(2)}) copy-start(f32[224,2304]{1,0:T(8,128)} %param.20) | copy-start | bytes 6193156
  7.2 61.2 %copy-start.17 = (f32[2,288,512]{2,1,0:T(8,128)S(1)}, f32[2,288,512]{2,1,0:T(8,128)}, u32[]{:S(2)}) copy-start(f32[2,288,512]{2,1,0:T(8,128)} %param.25) | copy-start | bytes 3538948
  7.2 79.7 %all-gather.10.cloned.1.call-start = ((), (), s32[]{:S(2)}) async-start(), calls=%async_computation.8 | async-start | bytes 2654208 | tf_op jit(solution)/shard_map/all_gather | solution.py:122
  17.9 90.5 %all-gather.8.cloned.1.call-start = ((), (), s32[]{:S(2)}) async-start(), calls=%async_computation.7 | async-start | bytes 5160960 | tf_op jit(solution)/shard_map/all_gather | solution.py:135
  62.6 19.3 copy-start.43
  62.6 21.1 copy-start.51
  64.5 19.3 copy-start.39
  65.0 224.0 %copy-start.34 = (f32[2304]{0:T(1024)}, f32[2304]{0:T(1024)S(1)}, u32[]{:S(2)}) copy-start(f32[2304]{0:T(1024)S(1)} %get-tuple-element.55) | copy-start | bytes 27652
  66.9 124.2 %all-gather.12.cloned.1.call-start = ((), (), s32[]{:S(2)}) async-start(), calls=%async_computation.9 | async-start | bytes 5308416 | tf_op jit(solution)/shard_map/all_gather | solution.py:121
  81.9 205.4 %reduce-scatter.8.cloned.1.call-start = ((), (), s32[]{:S(2)}) async-start(), calls=%async_computation.10 | async-start | bytes 10321920 | tf_op jit(solution)/shard_map/reduce_scatter | solution.py:171
  108.4 8.8 copy-start.58
  117.2 87.1 %copy-start.11 = (f32[896,256]{0,1:T(8,128)}, f32[896,256]{0,1:T(8,128)S(1)}, u32[]{:S(2)}) copy-start(f32[896,256]{0,1:T(8,128)S(1)} %get-tuple-element.52) | copy-start | bytes 2752516
  218.1 162.0 %all-gather.16.cloned.1.call-start = ((), (), s32[]{:S(2)}) async-start(), calls=%async_computation.12 | async-start | bytes 5160960 | tf_op jit(solution)/shard_map/all_gather | solution.py:176
  289.1 6.1 copy-start.54
  291.2 88.7 %copy-start.48 = (f32[224]{0:T(256)}, f32[224]{0:T(256)S(1)}, u32[]{:S(2)}) copy-start(f32[224]{0:T(256)S(1)} %get-tuple-element.36) | copy-start | bytes 2692
  293.8 692.2 %all-gather.14.cloned.1.call-start = ((), (), s32[]{:S(2)}) async-start(), calls=%async_computation.11 | async-start | bytes 35831808 | tf_op jit(solution)/shard_map/all_gather | solution.py:123
  380.0 728.4 %reduce-scatter.10.cloned.1.call-start = ((), (), s32[]{:S(2)}) async-start(), calls=%async_computation.13 | async-start | bytes 10321920 | tf_op jit(solution)/shard_map/reduce_scatter | solution.py:180
  1037.3 76.5 %copy-start.3 = (f32[224,2304]{1,0:T(8,128)S(1)}, f32[224,2304]{1,0:T(8,128)}, u32[]{:S(2)}) copy-start(f32[224,2304]{1,0:T(8,128)} %copy-done.2) | copy-start | bytes 6193156
  1037.3 113.4 %all-gather.18.cloned.1.call-start = ((), (), s32[]{:S(2)}) async-start(), calls=%async_computation.14 | async-start | bytes 5160960 | tf_op jit(solution)/shard_map/all_gather | solution.py:190
  1116.4 159.2 %reduce-scatter.12.cloned.1.call-start = ((), (), s32[]{:S(2)}) async-start(), calls=%async_computation.15 | async-start | bytes 10321920 | tf_op jit(solution)/shard_map/reduce_scatter | solution.py:209
  1204.6 73.3 %copy-start.49 = (f32[224]{0:T(256)S(1)}, f32[224]{0:T(256)}, u32[]{:S(2)}) copy-start(f32[224]{0:T(256)} %copy-done.48) | copy-start | bytes 2692
  1204.6 73.3 %copy-start.35 = (f32[2304]{0:T(1024)S(1)}, f32[2304]{0:T(1024)}, u32[]{:S(2)}) copy-start(f32[2304]{0:T(1024)} %copy-done.34) | copy-start | bytes 27652
  1204.6 73.3 %copy-start.42 = (f32[224]{0:T(256)S(1)}, f32[224]{0:T(256)}, u32[]{:S(2)}) copy-start(f32[224]{0:T(256)} %copy-done.41) | copy-start | bytes 2692
  1204.7 113.8 %all-gather.20.cloned.1.call-start = ((), (), s32[]{:S(2)}) async-start(), calls=%async_computation.16 | async-start | bytes 5160960 | tf_op jit(solution)/shard_map/all_gather | solution.py:220
  1284.1 39.9 %copy-start.15 = (pred[896,896]{0,1:T(8,128)(4,1)S(1)}, pred[896,896]{0,1:T(8,128)(4,1)}, u32[]{:S(2)}) copy-start(pred[896,896]{0,1:T(8,128)(4,1)} %fusion.70) | copy-start | bytes 2408452
  1284.2 39.9 %copy-start.38 = (f32[2,896]{1,0:T(2,128)S(1)}, f32[2,896]{1,0:T(2,128)}, u32[]{:S(2)}) copy-start(f32[2,896]{1,0:T(2,128)} %copy-done.37) | copy-start | bytes 21508
  1284.2 39.8 %copy-start.66 = (bf16[896,256,1]{1,0,2:T(8,128)(2,1)S(1)}, bf16[896,256,1]{1,0,2:T(8,128)(2,1)}, u32[]{:S(2)}) copy-start(bf16[896,256,1]{1,0,2:T(8,128)(2,1)} %fusion.98) | copy-start | bytes 1376260
  1284.2 164.3 %reduce-scatter.18.cloned.1.call-start = ((), (), s32[]{:S(2)}) async-start(), calls=%async_computation.19 | async-start | bytes 2654208 | tf_op jit(solution)/shard_map/reduce_scatter | solution.py:270
  1324.0 11.1 slice-start
  1324.0 11.0 slice-start.1
  1335.0 10.5 copy-start.30
  1338.0 7.5 copy-start.59
  1350.1 167.5 %reduce-scatter.16.cloned.1.call-start = ((), (), s32[]{:S(2)}) async-start(), calls=%async_computation.18 | async-start | bytes 5308416 | tf_op jit(solution)/shard_map/reduce_scatter | solution.py:264
  1363.8 227.2 %reduce-scatter.14.cloned.1.call-start = ((), (), s32[]{:S(2)}) async-start(), calls=%async_computation.17 | async-start | bytes 10321920 | tf_op jit(solution)/shard_map/reduce_scatter | solution.py:252
  1375.5 732.8 %reduce-scatter.20.cloned.1.call-start = ((), (), s32[]{:S(2)}) async-start(), calls=%async_computation.20 | async-start | bytes 35831808 | tf_op jit(solution)/shard_map/reduce_scatter | solution.py:276
  1375.6 20.8 copy-start.61
  1447.7 143.3 %copy-start.1 = (f32[224,2304]{1,0:T(8,128)S(1)}, f32[224,2304]{1,0:T(8,128)}, u32[]{:S(2)}) copy-start(f32[224,2304]{1,0:T(8,128)} %param.20) | copy-start | bytes 6193156
  1447.7 143.3 %copy-start.33 = (f32[2304]{0:T(1024)S(1)}, f32[2304]{0:T(1024)}, u32[]{:S(2)}) copy-start(f32[2304]{0:T(1024)} %copy-done.32) | copy-start | bytes 27652
  1447.7 143.3 %copy-start.40 = (f32[224]{0:T(256)S(1)}, f32[224]{0:T(256)}, u32[]{:S(2)}) copy-start(f32[224]{0:T(256)} %copy-done.39) | copy-start | bytes 2692
  1447.8 190.5 %copy-start.45 = (f32[224]{0:T(256)S(1)}, f32[224]{0:T(256)}, u32[]{:S(2)}) copy-start(f32[224]{0:T(256)} %copy-done.44) | copy-start | bytes 2692
  2114.3 44.4 %copy-start.50 = (f32[288]{0:T(512)S(1)}, f32[288]{0:T(512)}, u32[]{:S(2)}) copy-start(f32[288]{0:T(512)} %param.28) | copy-start | bytes 3460
  2114.4 44.4 %copy-start.52 = (f32[288]{0:T(512)S(1)}, f32[288]{0:T(512)}, u32[]{:S(2)}) copy-start(f32[288]{0:T(512)} %param.36) | copy-start | bytes 3460
  2114.4 44.4 %copy-start.53 = (f32[288]{0:T(512)S(1)}, f32[288]{0:T(512)}, u32[]{:S(2)}) copy-start(f32[288]{0:T(512)} %param.32) | copy-start | bytes 3460
  2118.4 45.7 %copy-start.23 = (f32[2,288,256]{2,1,0:T(8,128)S(1)}, f32[2,288,256]{2,1,0:T(8,128)}, u32[]{:S(2)}) copy-start(f32[2,288,256]{2,1,0:T(8,128)} %param.26) | copy-start | bytes 1769476
  2118.4 45.7 %copy-start.27 = (bf16[2,288,256]{2,1,0:T(8,128)(2,1)S(1)}, bf16[2,288,256]{2,1,0:T(8,128)(2,1)}, u32[]{:S(2)}) copy-start(bf16[2,288,256]{2,1,0:T(8,128)(2,1)} %reduce-scatter.18.cloned.1.call-done) | copy-start | bytes 884740
  2159.5 7.4 copy-start.10
  (37 other events, 107.1 us)
Sparse Core Ops, SparseCore 0:
  18.0 55.5 all-gather.9
  75.7 32.6 all-gather.7
  111.2 79.8 all-gather.11
  218.2 69.0 reduce-scatter.7
  293.9 34.1 all-gather.15
  380.1 605.7 all-gather.13
  1037.4 70.8 reduce-scatter.9
  1116.6 34.0 all-gather.17
  1204.7 70.9 reduce-scatter.11
  1284.3 34.0 all-gather.19
  1350.2 68.9 reduce-scatter.17
  1423.3 94.2 reduce-scatter.15
  1520.2 70.7 reduce-scatter.13
  1594.7 513.4 reduce-scatter.19
where the time goes:
time: 2200 us; the launch traced here: 2190 us
  waiting for transfers between devices  1590 us (72%)
  matrix products  218 us (10%)
  other arithmetic  212 us (10%)
  blocking collectives  128 us (6%)
  between operations  24.7 us (1%)
    all_gather x1, waiting for transfers between devices, local(): lax.all_gather(low_mlp, 'dp', axis=1, tiled=True)  606 us
    reduce_scatter x1, waiting for transfers between devices, local(): lax.psum_scatter(jnp.concatenate([grad_gate_up_w, grad_down[None]], 0).as...  470 us
    convert_element_type x3, other arithmetic, quantize(): ((sliced * spacing).astype(jnp.float32) * step_sizes).astype(jnp.bfloat16)  106 us
    unnamed x2, blocking collectives  88.2 us
    all_gather x1, waiting for transfers between devices, local(): lax.all_gather(low_qo, 'dp', axis=1, tiled=True)  71.8 us
    reduce_scatter x1, waiting for transfers between devices, local(): lax.psum_scatter(jnp.einsum('ktf,kdf->td', row_block, back_mlp[:2], prefe...  71 us
    reduce_scatter x1, waiting for transfers between devices, local(): lax.psum_scatter(contract_cols(row_block, full_mlp[2]), 'mp', scatter_dim...  70.9 us
    reduce_scatter x1, waiting for transfers between devices, local(): lax.psum_scatter(contract_cols(grad_query_lin, back_qo[0]) + contract_col...  70.1 us
  transfers between devices with their start and end apart: 14, of which 11 were waited for; matrix products, arithmetic and copies ran while one was open for 10% of the time, Pallas kernels for 0%

commit v1 on v0

--- a/solution.py
+++ b/solution.py
@@ -1,3 +1,4 @@
+import functools
 import math
 import jax
 import jax.numpy as jnp
@@ -20,6 +21,34 @@
 WEIGHT_DECAY = 0.1
 ADAM_EPSILON = 1e-08
 CLIP_SCALE = 0.5
+
+
+def make_values(arr, named_axis):
+    carry = lax.psum(1, axis_name=named_axis)
+    heard = lax.axis_index(named_axis)
+    earlier, later, answer = (carry, heard, arr.shape[1])
+    h_now = range(earlier)
+    leaves = list(map(lambda m: (m, (m + 1) % earlier), h_now))
+    v1 = map(lambda m: (m, (m - 1) % earlier), range(earlier))
+    heap = list(v1)
+    block_now = jnp.zeros((*arr.shape[:1], earlier * answer, *arr.shape[2:]), arr.dtype)
+    block_now = lax.dynamic_update_slice_in_dim(block_now, arr, later * answer, axis=1)
+    all_values = oldest = arr
+    v_now = earlier // 2
+    for ix in range(1, v_now + 1):
+        all_values = lax.ppermute(all_values, perm=leaves, axis_name=named_axis)
+        block_now = lax.dynamic_update_slice_in_dim(
+            block_now, all_values, (later - ix) % earlier * answer, axis=1
+        )
+        if ix < earlier - v_now:
+            oldest = lax.ppermute(oldest, axis_name=named_axis, perm=heap)
+            block_now = lax.dynamic_update_slice_in_dim(
+                block_now, oldest, (later + ix) % earlier * answer, axis=1
+            )
+    return block_now
+
+
+expand_the_stocks = functools.partial(make_values, named_axis="dp")
 
 
 def quantize(master, fan_list, selector):
@@ -118,7 +147,7 @@
     low_kv = quantize(w_kv, (D, D), bit_sel[1])
     low_mlp = quantize(w_mlp, (D, D, FF), bit_sel[2])
     full_qo, full_kv, full_mlp = (
-        lax.all_gather(low_qo, "dp", axis=1, tiled=True),
+        expand_the_stocks(low_qo),
         lax.all_gather(low_kv, "dp", axis=1, tiled=True),
         lax.all_gather(low_mlp, "dp", axis=1, tiled=True),
     )

time: 2200 us -> 2340 us (1.064)
  local copies, waits for them, and re-layouts: 20.8 us -> 106 us
  starting transfers between devices: 0.97 us -> 40.1 us
    dynamic_update_slice x0 -> x8, local copies, waits for them, and re-layouts: none -> 70.3 us  [the longest x4 35 us: make_values(): lax.dynamic_update_slice_in_dim(block_now, all_values, (later - ix) % ear...]
    ppermute x0 -> x7, waiting for transfers between devices: none -> 39.7 us  [the longest x4 39.7 us: make_values(): all_values = lax.ppermute(all_values, perm=leaves, axis_name=named_axis)]
    ppermute x0 -> x7, starting transfers between devices: none -> 39.1 us  [the longest x3 29.3 us: make_values(): oldest = lax.ppermute(oldest, axis_name=named_axis, perm=heap)]
  transfers between devices with their start and end apart: 14 -> 21, of which waited for: 11 -> 13; matrix products, arithmetic and copies ran while one was open for 10% -> 13% of each run, Pallas kernels for 0% -> 0%
where the time goes in v1:
time: 2340 us; the launch traced here: 2330 us
  waiting for transfers between devices  1610 us (69%)
  matrix products  217 us (9%)
  other arithmetic  210 us (9%)
  blocking collectives  128 us (5%)
  local copies, waits for them, and re-layouts  106 us (5%)
  starting transfers between devices  40.1 us (2%)
  between operations  24.9 us (1%)
    all_gather x1, waiting for transfers between devices, local(): lax.all_gather(low_mlp, 'dp', axis=1, tiled=True)  606 us
    reduce_scatter x1, waiting for transfers between devices, local(): lax.psum_scatter(jnp.concatenate([grad_gate_up_w, grad_down[None]], 0).as...  470 us
    convert_element_type x3, other arithmetic, quantize(): ((sliced * spacing).astype(jnp.float32) * step_sizes).astype(jnp.bfloat16)  106 us
    unnamed x2, blocking collectives  88.2 us
    all_gather x1, waiting for transfers between devices, local(): lax.all_gather(low_qo, 'dp', axis=1, tiled=True)  74.2 us
    reduce_scatter x1, waiting for transfers between devices, local(): lax.psum_scatter(contract_cols(row_block, full_mlp[2]), 'mp', scatter_dim...  70.8 us
    reduce_scatter x1, waiting for transfers between devices, local(): lax.psum_scatter(contract_cols(row_block, full_qo[1]), 'mp', scatter_dime...  70.6 us
    reduce_scatter x1, waiting for transfers between devices, local(): lax.psum_scatter(jnp.einsum('ktf,kdf->td', row_block, back_mlp[:2], prefe...  70.2 us
  transfers between devices with their start and end apart: 21, of which 13 were waited for; matrix products, arithmetic and copies ran while one was open for 13% of the time, Pallas kernels for 0%

profile of v1, /device:TPU:0, one launch (start us, length us, event | category | flops | bytes accessed | tf_op | source)
XLA Modules:
  0.0 2332.6 jit_solution(16436520585783709005)
XLA Ops:
  10.0 7.8 fusion.133
  18.9 43.8 %all-reduce.4 = f32[9216]{0:T(1024)S(1)} all-reduce(f32[9216]{0:T(1024)S(1)} %dynamic-update-slice), channel_id=1, replica_groups=mesh['dp'=8,'mp'=4] {'dp','mp'}, use_global_device_ids=true, to_apply=%add.4 | all-reduce | flops 9216 | bytes 73728
  67.9 13.7 fusion.105
  86.4 21.1 collective-permute-done
  111.3 12.2 collective-permute-start.3
  123.5 10.1 collective-permute-done.2
  136.8 14.6 collective-permute-start.5
  151.4 8.4 collective-permute-done.4
  165.3 7.9 dynamic_update_slice.24
  178.0 8.6 dynamic_update_slice.25
  188.8 9.1 dynamic_update_slice.26
  200.2 9.1 dynamic_update_slice.27
  211.5 9.1 dynamic_update_slice.28
  222.9 9.1 dynamic_update_slice.29
  234.2 9.1 dynamic_update_slice.30
  245.6 8.2 dynamic_update_slice.31
  257.0 4.1 fusion.113
  279.0 5.6 fusion.74
  284.7 70.6 %reduce-scatter.8.cloned.1.call-done = f32[224,2304]{1,0:T(8,128)} async-done(((f32[896,2304]{1,0:T(8,128)}), f32[224,2304]{1,0:T(8,128)}) %reduce-scatter.8.cloned.1.call-update) | async-done | bytes 2064400 | tf_op jit(solution)/shard_map/reduce_scatter | solution.py:200
  363.8 84.8 %fusion.33 = bf16[3,288,2304]{2,1,0:T(8,128)(2,1)} fusion(f32[3,288,2304]{2,1,0:T(8,128)} %param.27, f32[3]{0:T(128)S(1)} %copy-done.56, s32[]{:T(128)} %bitcast.23, s32[]{:T(128)S(6)} %sign.50, s32[]{:T(128)S(6)} %select_n.162, f32[3]{0:T(128)S(1)} %copy-done.57, s32[]{:T(128)S(6)} %neg.36, s32[]{:T(128)S(6)} %sub.146), kind=kLoop, calls=%fused_computation.52 | loop fusion | flops 39813120 | bytes 11943980 | tf_op jit(solution)/shard_map/convert_element_type | solution.py:63
  448.7 605.9 %all-gather.12.cloned.1.call-done = bf16[3,2304,2304]{2,1,0:T(8,128)(2,1)} async-done(((bf16[3,288,2304]{2,1,0:T(8,128)(2,1)}), bf16[3,2304,2304]{2,1,0:T(8,128)(2,1)}) %all-gather.12.cloned.1.call-update) | async-done | bytes 31850512 | tf_op jit(solution)/shard_map/all_gather | solution.py:152
  1054.5 28.8 %convolution_bitcast_fusion = f32[2,896,2304]{1,2,0:T(8,128)} fusion(bf16[3,2304,2304]{2,1,0:T(8,128)(2,1)} %all-gather.12.cloned.1.call-done, bf16[896,2304]{1,0:T(8,128)(2,1)} %all-gather.14.cloned.1.call-done), kind=kOutput, calls=%fused_computation.18 | convolution fusion | flops 19025362944 | bytes 52494336 | tf_op jit(solution)/shard_map/td,kdf->ktf/dot_general | solution.py:206
  1083.3 22.6 fusion.6
  1106.1 70.8 %reduce-scatter.10.cloned.1.call-done = f32[224,2304]{1,0:T(8,128)} async-done(((f32[896,2304]{1,0:T(8,128)}), f32[224,2304]{1,0:T(8,128)}) %reduce-scatter.10.cloned.1.call-update) | async-done | bytes 2064400 | tf_op jit(solution)/shard_map/reduce_scatter | solution.py:209
  1185.1 34.2 %all-gather.16.cloned.1.call-done = bf16[896,2304]{1,0:T(8,128)(2,1)} async-done(((bf16[224,2304]{1,0:T(8,128)(2,1)}), bf16[896,2304]{1,0:T(8,128)(2,1)}) %all-gather.16.cloned.1.call-update) | async-done | bytes 4128784 | tf_op jit(solution)/shard_map/all_gather | solution.py:219
  1219.3 26.8 %fusion.58 = (bf16[1,896,2304]{1,2,0:T(8,128)(2,1)}, bf16[1,896,2304]{1,2,0:T(8,128)(2,1)}) fusion(f32[2,896,2304]{1,2,0:T(8,128)} %convolution_bitcast_fusion, bf16[896,2304]{1,0:T(8,128)(2,1)} %all-gather.16.cloned.1.call-done, bf16[3,2304,2304]{2,1,0:T(8,128)(2,1)} %all-gather.12.cloned.1.call-done), kind=kOutput, calls=%fused_computation.87 | convolution fusion | flops 9562226688 | bytes 39518208 | tf_op jit(solution)/shard_map/dot_general | solution.py:225
  1246.1 27.1 %fusion.43 = f32[896,2304]{1,0:T(8,128)} fusion(bf16[3,2304,2304]{2,1,0:T(8,128)(2,1)} %all-gather.12.cloned.1.call-done, bf16[1,896,2304]{1,2,0:T(8,128)(2,1)} %get-tuple-element.39, bf16[1,896,2304]{1,2,0:T(8,128)(2,1)} %get-tuple-element.38), kind=kOutput, calls=%fused_computation.73 | convolution fusion | flops 19029491712 | bytes 37748736 | tf_op jit(solution)/shard_map/ktf,kdf->td/dot_general | solution.py:239
  1274.1 70.2 %reduce-scatter.12.cloned.1.call-done = f32[224,2304]{1,0:T(8,128)} async-done(((f32[896,2304]{1,0:T(8,128)}), f32[224,2304]{1,0:T(8,128)}) %reduce-scatter.12.cloned.1.call-update) | async-done | bytes 2064400 | tf_op jit(solution)/shard_map/reduce_scatter | solution.py:238
  1352.8 74.2 %all-gather.20.cloned.1.call-done = bf16[2,2304,512]{2,1,0:T(8,128)(2,1)} async-done(((bf16[2,288,512]{2,1,0:T(8,128)(2,1)}), bf16[2,2304,512]{2,1,0:T(8,128)(2,1)}) %all-gather.20.cloned.1.call-update) | async-done | bytes 4718608 | tf_op jit(solution)/shard_map/all_gather | solution.py:221
  1427.0 34.3 %all-gather.18.cloned.1.call-done = bf16[896,2304]{1,0:T(8,128)(2,1)} async-done(((bf16[224,2304]{1,0:T(8,128)(2,1)}), bf16[896,2304]{1,0:T(8,128)(2,1)}) %all-gather.18.cloned.1.call-update) | async-done | bytes 4128784 | tf_op jit(solution)/shard_map/all_gather | solution.py:249
  1461.3 5.6 fusion.84
  1466.9 5.5 fusion.41
  1472.4 5.4 fusion.97
  1480.8 3.8 fusion.124
  1510.1 4.2 fusion.72
  1514.3 4.5 add_add_fusion
  1518.9 20.8 fusion.3
  1539.7 29.3 %fusion.2 = bf16[2,2304,2304]{2,1,0:T(8,128)(2,1)} fusion(bf16[1,896,2304]{1,2,0:T(8,128)(2,1)} %get-tuple-element.39, bf16[1,896,2304]{1,2,0:T(8,128)(2,1)} %get-tuple-element.38, bf16[896,2304]{1,0:T(8,128)(2,1)S(1)} %copy-done.63), kind=kOutput, calls=%fused_computation.4 | convolution fusion | flops 19052494848 | bytes 33619968 | tf_op jit(solution)/shard_map/ktf,td->kdf/dot_general | solution.py:234
  1569.1 22.1 pad_maximum_fusion
  1593.6 66.7 %reduce-scatter.16.cloned.1.call-done = bf16[2,288,512]{2,1,0:T(8,128)(2,1)} async-done(((bf16[2,2304,512]{2,1,0:T(8,128)(2,1)}), bf16[2,288,512]{2,1,0:T(8,128)(2,1)}) %reduce-scatter.16.cloned.1.call-update) | async-done | bytes 589840 | tf_op jit(solution)/shard_map/reduce_scatter | solution.py:293
  1663.7 70.1 %reduce-scatter.14.cloned.1.call-done = f32[224,2304]{1,0:T(8,128)} async-done(((f32[896,2304]{1,0:T(8,128)}), f32[224,2304]{1,0:T(8,128)}) %reduce-scatter.14.cloned.1.call-update) | async-done | bytes 2064400 | tf_op jit(solution)/shard_map/reduce_scatter | solution.py:281
  1735.9 44.4 %all-reduce.5 = f32[9216]{0:T(1024)S(1)} all-reduce(f32[9216]{0:T(1024)S(1)} %reshape.540), channel_id=9, replica_groups=mesh['dp'=8,'mp'=4] {'dp','mp'}, use_global_device_ids=true, to_apply=%region_27.28.clone | all-reduce | flops 9216 | bytes 73728
  1781.0 470.1 %reduce-scatter.20.cloned.1.call-done = bf16[3,288,2304]{2,1,0:T(8,128)(2,1)} async-done(((bf16[3,2304,2304]{2,1,0:T(8,128)(2,1)}), bf16[3,288,2304]{2,1,0:T(8,128)(2,1)}) %reduce-scatter.20.cloned.1.call-update) | async-done | bytes 3981328 | tf_op jit(solution)/shard_map/reduce_scatter | solution.py:305
  2251.1 4.8 fusion.27
  2257.3 4.1 fusion.78
  2261.4 39.7 %psum.7 = f32[]{:T(128)} all-reduce(f32[]{:T(128)S(6)} %add.378), channel_id=1, replica_groups=mesh['dp'=8,'mp'=4] {'dp','mp'}, use_global_device_ids=true, to_apply=%region_29.30 | all-reduce | flops 1 | bytes 8 | tf_op jit(solution)/shard_map/psum | solution.py:322
  2302.5 4.1 multiply_subtract_fusion.1
  2308.1 16.3 multiply_subtract_fusion
  (271 shorter events, 124.2 us)
Async XLA Ops:
  7.2 60.7 %copy-start.58 = (f32[2]{0:T(128)S(1)}, f32[2]{0:T(128)}, u32[]{:S(2)}) copy-start(f32[2]{0:T(128)} %constant.277) | copy-start | bytes 28
  7.2 60.7 %copy-start.59 = (f32[2]{0:T(128)S(1)}, f32[2]{0:T(128)}, u32[]{:S(2)}) copy-start(f32[2]{0:T(128)} %constant.263.clone) | copy-start | bytes 28
  7.2 57.9 %copy-start = (f32[224,2304]{1,0:T(8,128)S(1)}, f32[224,2304]{1,0:T(8,128)}, u32[]{:S(2)}) copy-start(f32[224,2304]{1,0:T(8,128)} %param.20) | copy-start | bytes 6193156
  7.2 249.8 %all-gather.10.cloned.1.call-start = ((), (), s32[]{:S(2)}) async-start(), calls=%async_computation.8 | async-start | bytes 2654208 | tf_op jit(solution)/shard_map/all_gather | solution.py:151
  17.9 239.1 %all-gather.8.cloned.1.call-start = ((), (), s32[]{:S(2)}) async-start(), calls=%async_computation.7 | async-start | bytes 5160960 | tf_op jit(solution)/shard_map/all_gather | solution.py:164
  17.9 92.1 %copy-start.45 = (s32[1,896]{1,0:T(1,128)S(1)}, s32[1,896]{1,0:T(1,128)}, u32[]{:S(2)}) copy-start(s32[1,896]{1,0:T(1,128)} %param.22) | copy-start | bytes 10756
  18.9 117.9 %copy-start.53 = (s32[1,896]{1,0:T(1,128)S(1)}, s32[1,896]{1,0:T(1,128)}, u32[]{:S(2)}) copy-start(s32[1,896]{1,0:T(1,128)} %param.23) | copy-start | bytes 10756
  64.5 293.2 %copy-start.36 = (f32[2304]{0:T(1024)}, f32[2304]{0:T(1024)S(1)}, u32[]{:S(2)}) copy-start(f32[2304]{0:T(1024)S(1)} %get-tuple-element.55) | copy-start | bytes 27652
  66.3 289.0 %reduce-scatter.8.cloned.1.call-start = ((), (), s32[]{:S(2)}) async-start(), calls=%async_computation.9 | async-start | bytes 10321920 | tf_op jit(solution)/shard_map/reduce_scatter | solution.py:200
  81.6 91.6 %copy-start.17 = (bf16[2,288,512]{2,1,0:T(8,128)(2,1)}, bf16[2,288,512]{2,1,0:T(8,128)(2,1)S(1)}, u32[]{:S(2)}) copy-start(bf16[2,288,512]{2,1,0:T(8,128)(2,1)S(1)} %fusion.105) | copy-start | bytes 1769476
  81.6 25.9 %collective-permute-start = (bf16[2,288,512]{2,1,0:T(8,128)(2,1)S(1)}, bf16[2,288,512]{2,1,0:T(8,128)(2,1)}, u32[]{:S(2)}, u32[]{:S(2)}) collective-permute-start(bf16[2,288,512]{2,1,0:T(8,128)(2,1)S(1)} %fusion.105), channel_id=1, source_target_pairs={{0,4},{4,8},{8,12},{12,16},{16,20},{20,24},{24,28},{28,0},{1,5},{5... | collective-permute-start | bytes 1769480 | tf_op jit(solution)/shard_map/ppermute | solution.py:39
  83.9 27.3 %collective-permute-start.1 = (bf16[2,288,512]{2,1,0:T(8,128)(2,1)S(1)}, bf16[2,288,512]{2,1,0:T(8,128)(2,1)S(1)}, u32[]{:S(2)}, u32[]{:S(2)}) collective-permute-start(bf16[2,288,512]{2,1,0:T(8,128)(2,1)S(1)} %fusion.105), channel_id=1, source_target_pairs={{0,28},{4,0},{8,4},{12,8},{16,12},{20,16},{24,20},{28,24},{1,29},{... | collective-permute-start | bytes 1769480 | tf_op jit(solution)/shard_map/ppermute | solution.py:44
  107.5 26.2 %collective-permute-start.2 = (bf16[2,288,512]{2,1,0:T(8,128)(2,1)}, bf16[2,288,512]{2,1,0:T(8,128)(2,1)}, u32[]{:S(2)}, u32[]{:S(2)}) collective-permute-start(bf16[2,288,512]{2,1,0:T(8,128)(2,1)} %collective-permute-done), channel_id=1, source_target_pairs={{0,4},{4,8},{8,12},{12,16},{16,20},{20,24},{24,28},{28,0},{1,5},{5... | collective-permute-start | bytes 1769480 | tf_op jit(solution)/shard_map/ppermute | solution.py:39
  111.3 51.0 %copy-start.31 = (bf16[2,288,512]{2,1,0:T(8,128)(2,1)}, bf16[2,288,512]{2,1,0:T(8,128)(2,1)S(1)}, u32[]{:S(2)}) copy-start(bf16[2,288,512]{2,1,0:T(8,128)(2,1)S(1)} %collective-permute-done.1) | copy-start | bytes 1769476
  111.3 25.5 %collective-permute-start.3 = (bf16[2,288,512]{2,1,0:T(8,128)(2,1)S(1)}, bf16[2,288,512]{2,1,0:T(8,128)(2,1)}, u32[]{:S(2)}, u32[]{:S(2)}) collective-permute-start(bf16[2,288,512]{2,1,0:T(8,128)(2,1)S(1)} %collective-permute-done.1), channel_id=1, source_target_pairs={{0,28},{4,0},{8,4},{12,8},{16,12},{20,16},{24,20},{28,24},{1,29},{... | collective-permute-start | bytes 1769480 | tf_op jit(solution)/shard_map/ppermute | solution.py:44
  133.7 26.2 %collective-permute-start.4 = (bf16[2,288,512]{2,1,0:T(8,128)(2,1)}, bf16[2,288,512]{2,1,0:T(8,128)(2,1)}, u32[]{:S(2)}, u32[]{:S(2)}) collective-permute-start(bf16[2,288,512]{2,1,0:T(8,128)(2,1)} %collective-permute-done.2), channel_id=1, source_target_pairs={{0,4},{4,8},{8,12},{12,16},{16,20},{20,24},{24,28},{28,0},{1,5},{5... | collective-permute-start | bytes 1769480 | tf_op jit(solution)/shard_map/ppermute | solution.py:39
  136.8 95.2 %collective-permute-start.5 = (bf16[2,288,512]{2,1,0:T(8,128)(2,1)}, bf16[2,288,512]{2,1,0:T(8,128)(2,1)}, u32[]{:S(2)}, u32[]{:S(2)}) collective-permute-start(bf16[2,288,512]{2,1,0:T(8,128)(2,1)} %collective-permute-done.3), channel_id=1, source_target_pairs={{0,28},{4,0},{8,4},{12,8},{16,12},{20,16},{24,20},{28,24},{1,29},{... | collective-permute-start | bytes 1769480 | tf_op jit(solution)/shard_map/ppermute | solution.py:44
  159.8 83.6 %collective-permute-start.6 = (bf16[2,288,512]{2,1,0:T(8,128)(2,1)}, bf16[2,288,512]{2,1,0:T(8,128)(2,1)}, u32[]{:S(2)}, u32[]{:S(2)}) collective-permute-start(bf16[2,288,512]{2,1,0:T(8,128)(2,1)} %collective-permute-done.4), channel_id=1, source_target_pairs={{0,4},{4,8},{8,12},{12,16},{16,20},{20,24},{24,28},{28,0},{1,5},{5... | collective-permute-start | bytes 1769480 | tf_op jit(solution)/shard_map/ppermute | solution.py:39
  175.5 100.1 %copy-start.15 = (pred[896,896]{0,1:T(8,128)(4,1)}, pred[896,896]{0,1:T(8,128)(4,1)S(1)}, u32[]{:S(2)}) copy-start(pred[896,896]{0,1:T(8,128)(4,1)S(1)} %fusion.70) | copy-start | bytes 2408452
  284.6 164.0 %all-gather.14.cloned.1.call-start = ((), (), s32[]{:S(2)}) async-start(), calls=%async_computation.11 | async-start | bytes 5160960 | tf_op jit(solution)/shard_map/all_gather | solution.py:205
  359.8 88.7 %copy-start.50 = (f32[224]{0:T(256)}, f32[224]{0:T(256)S(1)}, u32[]{:S(2)}) copy-start(f32[224]{0:T(256)S(1)} %get-tuple-element.36) | copy-start | bytes 2692
  362.4 692.2 %all-gather.12.cloned.1.call-start = ((), (), s32[]{:S(2)}) async-start(), calls=%async_computation.10 | async-start | bytes 35831808 | tf_op jit(solution)/shard_map/all_gather | solution.py:152
  448.6 728.4 %reduce-scatter.10.cloned.1.call-start = ((), (), s32[]{:S(2)}) async-start(), calls=%async_computation.12 | async-start | bytes 10321920 | tf_op jit(solution)/shard_map/reduce_scatter | solution.py:209
  1106.0 76.5 %copy-start.3 = (f32[224,2304]{1,0:T(8,128)S(1)}, f32[224,2304]{1,0:T(8,128)}, u32[]{:S(2)}) copy-start(f32[224,2304]{1,0:T(8,128)} %copy-done.2) | copy-start | bytes 6193156
  1106.0 113.4 %all-gather.16.cloned.1.call-start = ((), (), s32[]{:S(2)}) async-start(), calls=%async_computation.13 | async-start | bytes 5160960 | tf_op jit(solution)/shard_map/all_gather | solution.py:219
  1185.1 159.2 %reduce-scatter.12.cloned.1.call-start = ((), (), s32[]{:S(2)}) async-start(), calls=%async_computation.14 | async-start | bytes 10321920 | tf_op jit(solution)/shard_map/reduce_scatter | solution.py:238
  1273.3 73.3 %copy-start.51 = (f32[224]{0:T(256)S(1)}, f32[224]{0:T(256)}, u32[]{:S(2)}) copy-start(f32[224]{0:T(256)} %copy-done.50) | copy-start | bytes 2692
  1273.3 73.3 %copy-start.37 = (f32[2304]{0:T(1024)S(1)}, f32[2304]{0:T(1024)}, u32[]{:S(2)}) copy-start(f32[2304]{0:T(1024)} %copy-done.36) | copy-start | bytes 27652
  1273.3 73.3 %copy-start.44 = (f32[224]{0:T(256)S(1)}, f32[224]{0:T(256)}, u32[]{:S(2)}) copy-start(f32[224]{0:T(256)} %copy-done.43) | copy-start | bytes 2692
  1273.3 153.7 %all-gather.20.cloned.1.call-start = ((), (), s32[]{:S(2)}) async-start(), calls=%async_computation.16 | async-start | bytes 5308416 | tf_op jit(solution)/shard_map/all_gather | solution.py:221
  1274.0 187.2 %all-gather.18.cloned.1.call-start = ((), (), s32[]{:S(2)}) async-start(), calls=%async_computation.15 | async-start | bytes 5160960 | tf_op jit(solution)/shard_map/all_gather | solution.py:249
  1352.8 114.1 %copy-start.16 = (pred[896,896]{0,1:T(8,128)(4,1)S(1)}, pred[896,896]{0,1:T(8,128)(4,1)}, u32[]{:S(2)}) copy-start(pred[896,896]{0,1:T(8,128)(4,1)} %copy-done.15) | copy-start | bytes 2408452
  1352.8 114.1 %copy-start.40 = (f32[2,896]{1,0:T(2,128)S(1)}, f32[2,896]{1,0:T(2,128)}, u32[]{:S(2)}) copy-start(f32[2,896]{1,0:T(2,128)} %copy-done.39) | copy-start | bytes 21508
  1352.8 114.1 %copy-start.68 = (bf16[896,256,1]{1,0,2:T(8,128)(2,1)S(1)}, bf16[896,256,1]{1,0,2:T(8,128)(2,1)}, u32[]{:S(2)}) copy-start(bf16[896,256,1]{1,0,2:T(8,128)(2,1)} %copy-done.67) | copy-start | bytes 1376260
  1352.8 239.1 %reduce-scatter.18.cloned.1.call-start = ((), (), s32[]{:S(2)}) async-start(), calls=%async_computation.19 | async-start | bytes 2654208 | tf_op jit(solution)/shard_map/reduce_scatter | solution.py:299
  1492.9 167.5 %reduce-scatter.16.cloned.1.call-start = ((), (), s32[]{:S(2)}) async-start(), calls=%async_computation.18 | async-start | bytes 5308416 | tf_op jit(solution)/shard_map/reduce_scatter | solution.py:293
  1507.2 226.5 %reduce-scatter.14.cloned.1.call-start = ((), (), s32[]{:S(2)}) async-start(), calls=%async_computation.17 | async-start | bytes 10321920 | tf_op jit(solution)/shard_map/reduce_scatter | solution.py:281
  1518.9 732.3 %reduce-scatter.20.cloned.1.call-start = ((), (), s32[]{:S(2)}) async-start(), calls=%async_computation.20 | async-start | bytes 35831808 | tf_op jit(solution)/shard_map/reduce_scatter | solution.py:305
  1591.1 142.6 %copy-start.1 = (f32[224,2304]{1,0:T(8,128)S(1)}, f32[224,2304]{1,0:T(8,128)}, u32[]{:S(2)}) copy-start(f32[224,2304]{1,0:T(8,128)} %param.20) | copy-start | bytes 6193156
  1591.1 142.6 %copy-start.35 = (f32[2304]{0:T(1024)S(1)}, f32[2304]{0:T(1024)}, u32[]{:S(2)}) copy-start(f32[2304]{0:T(1024)} %copy-done.34) | copy-start | bytes 27652
  1591.2 142.6 %copy-start.42 = (f32[224]{0:T(256)S(1)}, f32[224]{0:T(256)}, u32[]{:S(2)}) copy-start(f32[224]{0:T(256)} %copy-done.41) | copy-start | bytes 2692
  1591.2 189.8 %copy-start.47 = (f32[224]{0:T(256)S(1)}, f32[224]{0:T(256)}, u32[]{:S(2)}) copy-start(f32[224]{0:T(256)} %copy-done.46) | copy-start | bytes 2692
  2257.2 44.6 %copy-start.52 = (f32[288]{0:T(512)S(1)}, f32[288]{0:T(512)}, u32[]{:S(2)}) copy-start(f32[288]{0:T(512)} %param.28) | copy-start | bytes 3460
  2257.2 45.3 %copy-start.18 = (f32[2,288,512]{2,1,0:T(8,128)S(1)}, f32[2,288,512]{2,1,0:T(8,128)}, u32[]{:S(2)}) copy-start(f32[2,288,512]{2,1,0:T(8,128)} %param.25) | copy-start | bytes 3538948
  2261.4 45.3 %copy-start.25 = (f32[2,288,256]{2,1,0:T(8,128)S(1)}, f32[2,288,256]{2,1,0:T(8,128)}, u32[]{:S(2)}) copy-start(f32[2,288,256]{2,1,0:T(8,128)} %param.26) | copy-start | bytes 1769476
  2261.4 45.3 %copy-start.28 = (bf16[2,288,256]{2,1,0:T(8,128)(2,1)S(1)}, bf16[2,288,256]{2,1,0:T(8,128)(2,1)}, u32[]{:S(2)}) copy-start(bf16[2,288,256]{2,1,0:T(8,128)(2,1)} %reduce-scatter.18.cloned.1.call-done) | copy-start | bytes 884740
  2261.4 45.3 %copy-start.29 = (f32[2,288,256]{2,1,0:T(8,128)S(1)}, f32[2,288,256]{2,1,0:T(8,128)}, u32[]{:S(2)}) copy-start(f32[2,288,256]{2,1,0:T(8,128)} %param.34) | copy-start | bytes 1769476
  2261.4 45.3 %copy-start.30 = (f32[2,288,256]{2,1,0:T(8,128)S(1)}, f32[2,288,256]{2,1,0:T(8,128)}, u32[]{:S(2)}) copy-start(f32[2,288,256]{2,1,0:T(8,128)} %param.30) | copy-start | bytes 1769476
  (46 other events, 262.2 us)
Sparse Core Ops, SparseCore 0:
  18.0 55.5 all-gather.9
  75.8 32.6 all-gather.7
  284.8 70.5 reduce-scatter.7
  362.5 34.2 all-gather.13
  448.7 605.7 all-gather.11
  1106.1 70.8 reduce-scatter.9
  1185.2 34.1 all-gather.15
  1273.4 70.8 reduce-scatter.11
  1347.1 79.8 all-gather.19
  1429.0 32.2 all-gather.17
  1493.0 68.9 reduce-scatter.17
  1566.1 94.2 reduce-scatter.15
  1663.0 70.6 reduce-scatter.13
  1737.5 513.5 reduce-scatter.19
